TPU v7x, 32 devices: a whole 2x2x4 slice. The times are simulated.
32 devices in a mesh: seq: 8 (over y, x, core), ch: 4 (over z).
Axes of the slice: x: 2, y: 2, z: 4, core: 2. Of those that a mesh axis runs over, the one named last changes fastest.
Arguments:
- inputs: bfloat16 [1536, 131072], P('ch', 'seq'), may hold values from -6 to 6
- gating: bfloat16 [1536, 131072], P('ch', 'seq'), may hold values from -6 to 6
- upstream: bfloat16 [1536, 131072], P('ch', 'seq'), may hold values from -6 to 6
- factor_one: bfloat16 [512, 512], replicated, may hold values from -0.25 to 0.25
- factor_two: bfloat16 [256, 256], replicated, may hold values from -0.375 to 0.375
- factor_three: bfloat16 [256, 256], replicated, may hold values from -0.375 to 0.375
- factor_four: bfloat16 [512, 512], replicated, may hold values from -0.25 to 0.25
- kernel_cols: float32 [1536, 512], P('ch'), may hold values from -4 to 4
- kernel_rows: float32 [1536, 256], P('ch'), may hold values from -4 to 4
Outputs:
- input_grad: bfloat16 [1536, 131072], P('ch', 'seq')
- gating_grad: bfloat16 [1536, 131072], P('ch', 'seq')
- one_grad: float32 [512, 512], replicated
- two_grad: float32 [256, 256], replicated
- three_grad: float32 [256, 256], replicated
- four_grad: float32 [512, 512], replicated
- cols_grad: float32 [1536, 512], P('ch')
- rows_grad: float32 [1536, 256], P('ch')
All inputs are finite; a program needn't handle non-finite values.
Results may differ from a plain program's by a relative error of at most 0.0076.
Values may be sent and summed in bfloat16 or wider, within the bound.
A program may use at most 384 MiB of HBM per device.

v0:
```python
import math
import jax
import jax.numpy as jnp
from jax import lax
from jax.sharding import PartitionSpec as P

P1 = 256
P2 = 512
C = 1536


def local(
    inputs,
    gating,
    upstream,
    factor_one,
    factor_two,
    factor_three,
    factor_four,
    kernel_cols,
    kernel_rows,
):
    width = inputs.shape[0]
    length = inputs.shape[1]
    parts = lax.axis_size("seq")
    flt = jnp.float32
    half = jnp.bfloat16
    rows_local = length // P2
    up_gate = (upstream.astype(flt) * gating.astype(flt)).astype(half)
    moved_in, moved_gate = (
        lax.all_to_all(inputs, "seq", split_axis=0, concat_axis=1, tiled=True),
        lax.all_to_all(up_gate, "seq", split_axis=0, concat_axis=1, tiled=True),
    )
    several = width // parts
    offset = lax.axis_index("seq") * several
    local_cols = lax.dynamic_slice_in_dim(kernel_cols, offset, several, 0)
    local_rows = lax.dynamic_slice_in_dim(kernel_rows, offset, several, 0)
    shaped = moved_in.reshape(several, P1, P2)
    gate_rows = moved_gate.reshape(several, P1, P2)
    first_prod = jnp.einsum("cij,jk->cik", shaped, factor_one, preferred_element_type=flt)
    first_out = (first_prod * local_cols[:, None, :]).astype(half)
    left_prod = jnp.einsum("ki,cij->ckj", factor_two, first_out, preferred_element_type=flt)
    left_out = (left_prod * local_rows[:, :, None]).astype(half)
    second = jnp.einsum("ki,cij->ckj", factor_three, left_out, preferred_element_type=flt).astype(
        half
    )
    grad_four = jnp.einsum("cij,cik->jk", second, gate_rows, preferred_element_type=flt)
    grad_second = jnp.einsum(
        "cik,jk->cij", gate_rows, factor_four, preferred_element_type=flt
    ).astype(half)
    grad_three = jnp.einsum("ckj,cij->ki", grad_second, left_out, preferred_element_type=flt)
    grad_left = jnp.einsum("ki,ckj->cij", factor_three, grad_second, preferred_element_type=flt)
    rows_part = jnp.sum(grad_left * left_prod, axis=2)
    grad_prod = (grad_left * local_rows[:, :, None]).astype(half)
    grad_two = jnp.einsum("ckj,cij->ki", grad_prod, first_out, preferred_element_type=flt)
    grad_first = jnp.einsum(
        "ki,ckj->cij", factor_two, grad_prod, preferred_element_type=flt
    ).astype(half)
    cols_part = jnp.sum(grad_first.astype(flt) * first_prod, axis=1)
    grad_inner = (grad_first.astype(flt) * local_cols[:, None, :]).astype(half)
    grad_one = jnp.einsum("cij,cik->jk", shaped, grad_inner, preferred_element_type=flt)
    local_input = jnp.einsum(
        "cik,jk->cij", grad_inner, factor_one, preferred_element_type=flt
    ).astype(half)
    input_grad, second_rows = (
        lax.all_to_all(
            local_input.reshape(several, P1 * P2), "seq", split_axis=1, concat_axis=0, tiled=True
        ),
        lax.all_to_all(
            second.reshape(several, P1 * P2), "seq", split_axis=1, concat_axis=0, tiled=True
        ),
    )
    cols_sum, rows_sum = (
        lax.all_gather(cols_part, "seq", axis=0, tiled=True),
        lax.all_gather(rows_part, "seq", axis=0, tiled=True),
    )
    final_prod = jnp.einsum(
        "cij,jk->cik",
        second_rows.reshape(width, rows_local, P2),
        factor_four,
        preferred_element_type=flt,
    )
    gating_grad = (
        (upstream.reshape(width, rows_local, P2).astype(flt) * final_prod)
        .astype(half)
        .reshape(width, length)
    )
    one_sum, two_sum, three_sum, four_sum = lax.psum(
        (grad_one, grad_two, grad_three, grad_four), ("seq", "ch")
    )
    scale_one = 1.0 / math.sqrt(P1 * C)
    scale_two = 1.0 / math.sqrt(P2 * C)
    return (
        input_grad,
        gating_grad,
        one_sum * scale_one,
        two_sum * scale_two,
        three_sum * scale_two,
        four_sum * scale_one,
        cols_sum / math.sqrt(P1),
        rows_sum / math.sqrt(P2),
    )


def solution(mesh):
    in_specs = (
        P("ch", "seq"),
        P("ch", "seq"),
        P("ch", "seq"),
        P(),
        P(),
        P(),
        P(),
        P("ch", None),
        P("ch", None),
    )
    out_specs = (P("ch", "seq"), P("ch", "seq"), P(), P(), P(), P(), P("ch", None), P("ch", None))
    return jax.shard_map(local, mesh=mesh, in_specs=in_specs, out_specs=out_specs, check_vma=False)
```

profile of v0, /device:TPU:0, one launch (start us, length us, event | category | flops | bytes accessed | tf_op | source)
XLA Modules:
  0.0 879.9 jit_solution(3477879930901490185)
XLA Ops:
  7.2 0.0 copy-start
  7.2 9.9 %multiply_convert_fusion.4 = bf16[384,16384]{1,0:T(8,128)(2,1)S(1)} fusion(bf16[384,16384]{1,0:T(8,128)(2,1)} %param.10, bf16[384,16384]{1,0:T(8,128)(2,1)} %param.11), kind=kLoop, calls=%fused_computation.9 | loop fusion | flops 25165824 | bytes 37748736 | tf_op jit(solution)/shard_map/convert_element_type | solution.py:29
  17.1 144.0 %all_to_all.67 = bf16[8,48,16384]{2,1,0:T(8,128)(2,1)} all-to-all(bf16[8,48,16384]{2,1,0:T(8,128)(2,1)S(1)} %bitcast.84), channel_id=1, replica_groups=mesh['seq'=8,'ch'=4] {'seq'}, dimensions={0} | all-to-all | bytes 25165824 | tf_op jit(solution)/shard_map/all_to_all | solution.py:32
  161.1 5.4 all-to-all-start.2
  166.5 0.8 constant_dynamic-slice_fusion.1
  167.3 14.4 %copy.71 = bf16[48,8,16384]{2,1,0:T(8,128)(2,1)} copy(bf16[48,8,16384]{2,0,1:T(8,128)(2,1)} %bitcast.82) | data formatting | bytes 25165824 | tf_op jit(solution)/shard_map/all_to_all | solution.py:32
  181.7 19.5 %reshape.52 = bf16[48,256,512]{2,1,0:T(8,128)(2,1)} reshape(bf16[48,8,16384]{2,1,0:T(8,128)(2,1)} %copy.71) | data formatting | bytes 25165824 | tf_op jit(solution)/shard_map/reshape | solution.py:39
  201.3 11.6 %convolution_convert_fusion.1 = bf16[48,256,512]{2,1,0:T(8,128)(2,1)S(1)} fusion(bf16[48,256,512]{2,1,0:T(8,128)(2,1)} %reshape.52, bf16[512,512]{1,0:T(8,128)(2,1)S(1)} %copy-done.4), kind=kOutput, calls=%fused_computation.19 | convolution fusion | flops 6448742400 | bytes 25690112 | tf_op jit(solution)/shard_map/cik,jk->cij/dot_general | solution.py:48
  212.8 4.5 copy-done.2
  217.4 10.1 %fusion.39 = f32[48,512,256]{2,1,0:T(8,128)} fusion(bf16[48,256,512]{2,1,0:T(8,128)(2,1)S(1)} %convolution_convert_fusion.1, bf16[256,256]{1,0:T(8,128)(2,1)S(1)} %copy-done.7), kind=kOutput, calls=%fused_computation.39 | convolution fusion | flops 3221225472 | bytes 37879808 | tf_op jit(solution)/shard_map/ki,ckj->cij/dot_general | solution.py:52
  227.5 14.8 %convolution_convert_fusion = bf16[48,512,256]{1,2,0:T(8,128)(2,1)} fusion(f32[48,512,256]{2,1,0:T(8,128)} %fusion.39, f32[48,256]{1,0:T(8,128)S(1)} %constant_dynamic-slice_fusion.1, bf16[256,256]{1,0:T(8,128)(2,1)S(1)} %copy-done.6), kind=kOutput, calls=%fused_computation.17 | convolution fusion | flops 3240099840 | bytes 37928960 | tf_op jit(solution)/shard_map/ki,ckj->cij/dot_general | solution.py:56
  242.3 14.4 %fusion.10 = bf16[48,256,512]{2,1,0:T(8,128)(2,1)} fusion(bf16[48,512,256]{1,2,0:T(8,128)(2,1)} %convolution_convert_fusion, f32[48,512]{1,0:T(8,128)S(1)} %constant_dynamic-slice_fusion, bf16[512,512]{1,0:T(8,128)(2,1)S(1)} %copy-done.3), kind=kOutput, calls=%fused_computation.18 | convolution fusion | flops 6467616768 | bytes 25788416 | tf_op jit(solution)/shard_map/cik,jk->cij/dot_general | solution.py:62
  256.7 19.8 %all_to_all.53 = bf16[48,8,16384]{2,1,0:T(8,128)(2,1)} reshape(bf16[48,256,512]{2,1,0:T(8,128)(2,1)} %fusion.10) | data formatting | bytes 25165824 | tf_op jit(solution)/shard_map/all_to_all | solution.py:66
  276.5 14.5 %copy.75 = bf16[48,8,16384]{2,0,1:T(8,128)(2,1)} copy(bf16[48,8,16384]{2,1,0:T(8,128)(2,1)} %all_to_all.53) | data formatting | bytes 25165824 | tf_op jit(solution)/shard_map/all_to_all | solution.py:66
  291.0 14.5 %all-to-all-done.2 = bf16[8,48,16384]{2,1,0:T(8,128)(2,1)} async-done(((bf16[8,48,16384]{2,1,0:T(8,128)(2,1)}), bf16[8,48,16384]{2,1,0:T(8,128)(2,1)}, u32[]{:S(2)}, u32[]{:S(2)}) %all-to-all-start.2) | async-done | bytes 12582944 | tf_op jit(solution)/shard_map/all_to_all | solution.py:31
  305.4 5.3 all-to-all-start.1
  310.8 17.6 %copy.76 = f32[384,16384]{0,1:T(8,128)} copy(bf16[384,16384]{1,0:T(8,128)(2,1)} %param.11) | data formatting | bytes 37748736 | tf_op jit(solution)/shard_map/convert_element_type | solution.py:29
  328.4 24.6 %copy.82 = f32[384,32,512]{2,0,1:T(8,128)} copy(f32[384,32,512]{0,2,1:T(8,128)} %bitcast.80) | data formatting | bytes 50331648 | tf_op jit(solution)/shard_map/convert_element_type | solution.py:84
  353.0 14.4 %copy.77 = bf16[48,8,16384]{2,1,0:T(8,128)(2,1)} copy(bf16[48,8,16384]{2,0,1:T(8,128)(2,1)} %bitcast.12) | data formatting | bytes 25165824 | tf_op jit(solution)/shard_map/all_to_all | solution.py:31
  367.4 19.5 %reshape.53 = bf16[48,256,512]{2,1,0:T(8,128)(2,1)} reshape(bf16[48,8,16384]{2,1,0:T(8,128)(2,1)} %copy.77) | data formatting | bytes 25165824 | tf_op jit(solution)/shard_map/reshape | solution.py:38
  387.0 18.9 %fusion.1 = (f32[48,512]{1,0:T(8,128)}, f32[48,256,512]{2,1,0:T(8,128)}) fusion(bf16[48,512,256]{1,2,0:T(8,128)(2,1)} %convolution_convert_fusion, bf16[48,256,512]{2,1,0:T(8,128)(2,1)} %reshape.53, bf16[512,512]{1,0:T(8,128)(2,1)S(1)} %copy-done.3), kind=kOutput, calls=%fused_computation.3 | convolution fusion | flops 6461300736 | bytes 50954240 | tf_op jit(solution)/shard_map/cij,jk->cik/dot_general | solution.py:40
  405.9 16.3 %fusion.21 = f32[48,512,256]{2,1,0:T(8,128)} fusion(f32[48,256,512]{2,1,0:T(8,128)} %get-tuple-element.45, f32[48,512]{1,0:T(8,128)S(1)} %constant_dynamic-slice_fusion, bf16[256,256]{1,0:T(8,128)(2,1)S(1)} %copy-done.6), kind=kOutput, calls=%fused_computation.22 | convolution fusion | flops 3233808384 | bytes 50561024 | tf_op jit(solution)/shard_map/ki,cij->ckj/dot_general | solution.py:42
  422.2 14.5 %convert_bitcast_fusion = bf16[48,256,512]{1,2,0:T(8,128)(2,1)} fusion(f32[48,512,256]{2,1,0:T(8,128)} %fusion.21, f32[48,256]{1,0:T(8,128)S(1)} %constant_dynamic-slice_fusion.1, bf16[256,256]{1,0:T(8,128)(2,1)S(1)} %copy-done.7), kind=kOutput, calls=%fused_computation.14 | convolution fusion | flops 3240099840 | bytes 37928960 | tf_op jit(solution)/shard_map/ki,cij->ckj/dot_general | solution.py:44
  436.7 16.7 %copy.79 = bf16[48,256,512]{2,1,0:T(8,128)(2,1)} copy(bf16[48,256,512]{1,2,0:T(8,128)(2,1)} %convert_bitcast_fusion) | data formatting | bytes 25165824 | tf_op jit(solution)/shard_map/convert_element_type | solution.py:44
  453.4 19.5 %all_to_all.60 = bf16[48,8,16384]{2,1,0:T(8,128)(2,1)} reshape(bf16[48,256,512]{2,1,0:T(8,128)(2,1)} %copy.79) | data formatting | bytes 25165824 | tf_op jit(solution)/shard_map/all_to_all | solution.py:69
  472.9 26.0 %copy.80 = bf16[48,8,16384]{2,0,1:T(8,128)(2,1)} copy(bf16[48,8,16384]{2,1,0:T(8,128)(2,1)} %all_to_all.60) | data formatting | bytes 25165824 | tf_op jit(solution)/shard_map/all_to_all | solution.py:69
  499.0 16.0 %fusion.28 = f32[256,256]{1,0:T(8,128)} fusion(bf16[48,256,512]{2,1,0:T(8,128)(2,1)} %copy-done.2, f32[48,512,256]{2,1,0:T(8,128)} %fusion.21, f32[48,256]{1,0:T(8,128)S(1)} %constant_dynamic-slice_fusion.1), kind=kOutput, calls=%fused_computation.26 | convolution fusion | flops 3233808384 | bytes 38060032 | tf_op jit(solution)/shard_map/ckj,cij->ki/dot_general | solution.py:51
  514.9 5.3 all-to-all-start.3
  520.3 0.0 all-reduce.3.cloned.1.call-start
  520.3 14.1 %fusion.22 = f32[512,512]{0,1:T(8,128)} fusion(bf16[48,256,512]{2,1,0:T(8,128)(2,1)} %reshape.53, bf16[48,512,256]{1,2,0:T(8,128)(2,1)} %convolution_convert_fusion, f32[48,512]{1,0:T(8,128)S(1)} %constant_dynamic-slice_fusion), kind=kOutput, calls=%fused_computation.23 | convolution fusion | flops 6461325312 | bytes 26312704 | tf_op jit(solution)/shard_map/cij,cik->jk/dot_general | solution.py:61
  534.4 12.6 %convolution_bitcast_fusion = f32[512,512]{0,1:T(8,128)} fusion(bf16[48,256,512]{1,2,0:T(8,128)(2,1)} %convert_bitcast_fusion, bf16[48,256,512]{2,1,0:T(8,128)(2,1)} %reshape.52), kind=kOutput, calls=%fused_computation.24 | convolution fusion | flops 6442450944 | bytes 26214400 | tf_op jit(solution)/shard_map/cij,cik->jk/dot_general | solution.py:47
  547.0 17.6 %fusion.25 = f32[256,256]{1,0:T(8,128)} fusion(f32[48,256,512]{2,1,0:T(8,128)} %get-tuple-element.45, f32[48,512]{1,0:T(8,128)S(1)} %constant_dynamic-slice_fusion, f32[48,512,256]{2,1,0:T(8,128)} %fusion.39, f32[48,256]{1,0:T(8,128)S(1)} %constant_dynamic-slice_fusion.1), kind=kOutput, calls=%fused_computation.25 | convolution fusion | flops 3246391296 | bytes 50741248 | tf_op jit(solution)/shard_map/ckj,cij->ki/dot_general | solution.py:55
  564.6 0.0 all-reduce.3.cloned.1.call-update
  564.6 16.7 %multiply_reduce_fusion = f32[48,256]{1,0:T(8,128)S(1)} fusion(f32[48,512,256]{2,1,0:T(8,128)} %fusion.39, f32[48,512,256]{2,1,0:T(8,128)} %fusion.21), kind=kLoop, calls=%fused_computation.4 | loop fusion | flops 12570624 | bytes 50380800 | tf_op jit(solution)/shard_map/reduce_sum | solution.py:53
  581.3 89.7 %all_gather.7 = f32[384,256]{1,0:T(8,128)S(1)} all-gather(f32[48,256]{1,0:T(8,128)S(1)} %multiply_reduce_fusion), channel_id=1, replica_groups=mesh['seq'=8,'ch'=4] {'seq'}, dimensions={0}, use_global_device_ids=true | all-gather | bytes 442368 | tf_op jit(solution)/shard_map/all_gather | solution.py:75
  671.0 9.2 %all_gather.6 = f32[384,512]{1,0:T(8,128)S(1)} all-gather(f32[48,512]{1,0:T(8,128)S(1)} %copy-done.8), channel_id=1, replica_groups=mesh['seq'=8,'ch'=4] {'seq'}, dimensions={0}, use_global_device_ids=true | all-gather | bytes 884736 | tf_op jit(solution)/shard_map/all_gather | solution.py:74
  680.2 0.8 broadcast_multiply_fusion.3
  681.0 0.9 broadcast_multiply_fusion.2
  682.0 62.6 %all-reduce.3.cloned.1.call-done = (f32[512,512]{0,1:T(8,128)}, f32[256,256]{1,0:T(8,128)}, f32[256,256]{1,0:T(8,128)}, f32[512,512]{0,1:T(8,128)}) async-done(((f32[512,512]{0,1:T(8,128)}, f32[256,256]{1,0:T(8,128)}, f32[256,256]{1,0:T(8,128)}, f32[512,512]{0,1:T(8,128)}), (f32[512,512]{0,1:T(8,128)}, f32[256,256]{1,0:T(8,128)}, f32[256,256]{1,0:T(8,128)}, ...) | async-done | bytes 2621456 | tf_op jit(solution)/shard_map/psum | solution.py:88
  744.5 1.8 broadcast_multiply_fusion
  746.3 1.3 copy.90
  747.6 1.3 copy.89
  748.9 1.9 broadcast_multiply_fusion.4
  750.8 12.8 %copy.101 = bf16[48,8,32,512]{3,2,1,0:T(8,128)(2,1)} copy(bf16[48,8,32,512]{3,1,2,0:T(8,128)(2,1)} %bitcast.26) | data formatting | bytes 25165824
  763.6 65.3 %multiply_convert_fusion = bf16[384,32,512]{2,0,1:T(8,128)(2,1)} fusion(f32[384,32,512]{2,0,1:T(8,128)} %copy.82, bf16[384,32,512]{2,1,0:T(8,128)(2,1)} %bitcast.81, bf16[512,512]{1,0:T(8,128)(2,1)S(1)} %copy-done.5), kind=kOutput, calls=%fused_computation.5 | convolution fusion | flops 6455033856 | bytes 50855936 | tf_op jit(solution)/shard_map/cij,jk->cik/dot_general | solution.py:77
  828.9 16.7 %copy.83 = bf16[384,32,512]{0,2,1:T(8,128)(2,1)} copy(bf16[384,32,512]{2,0,1:T(8,128)(2,1)} %multiply_convert_fusion) | data formatting | bytes 25165824 | tf_op jit(solution)/shard_map/convert_element_type | solution.py:85
  845.6 16.6 %copy.88 = bf16[384,16384]{1,0:T(8,128)(2,1)} copy(bf16[384,16384]{0,1:T(8,128)(2,1)} %bitcast.83) | data formatting | bytes 25165824
  862.2 10.5 %copy.111 = bf16[384,16384]{1,0:T(8,128)(2,1)} copy(bf16[384,16384]{1,0:T(8,128)(2,1)} %bitcast.9) | data formatting | bytes 25165824
  (19 shorter events, 0.0 us)
Async XLA Ops:
  7.2 160.1 %copy-start = (f32[384,512]{1,0:T(8,128)S(1)}, f32[384,512]{1,0:T(8,128)}, u32[]{:S(2)}) copy-start(f32[384,512]{1,0:T(8,128)} %param.16) | copy-start | bytes 2359300
  161.1 144.4 %all-to-all-start.2 = ((bf16[8,48,16384]{2,1,0:T(8,128)(2,1)}), bf16[8,48,16384]{2,1,0:T(8,128)(2,1)}, u32[]{:S(2)}, u32[]{:S(2)}) async-start(bf16[8,48,16384]{2,1,0:T(8,128)(2,1)} %bitcast.85), calls=%async_computation.2 | async-start | bytes 25165824 | tf_op jit(solution)/shard_map/all_to_all | solution.py:31
  181.7 19.5 %copy-start.4 = (bf16[512,512]{1,0:T(8,128)(2,1)S(1)}, bf16[512,512]{1,0:T(8,128)(2,1)}, u32[]{:S(2)}) copy-start(bf16[512,512]{1,0:T(8,128)(2,1)} %param.15) | copy-start | bytes 1572868
  201.3 16.1 %copy-start.7 = (bf16[256,256]{1,0:T(8,128)(2,1)S(1)}, bf16[256,256]{1,0:T(8,128)(2,1)}, u32[]{:S(2)}) copy-start(bf16[256,256]{1,0:T(8,128)(2,1)} %param.14) | copy-start | bytes 393220
  212.8 4.5 copy-start.2
  217.4 10.1 %copy-start.6 = (bf16[256,256]{1,0:T(8,128)(2,1)S(1)}, bf16[256,256]{1,0:T(8,128)(2,1)}, u32[]{:S(2)}) copy-start(bf16[256,256]{1,0:T(8,128)(2,1)} %param.13) | copy-start | bytes 393220
  227.5 14.8 %copy-start.3 = (bf16[512,512]{1,0:T(8,128)(2,1)S(1)}, bf16[512,512]{1,0:T(8,128)(2,1)}, u32[]{:S(2)}) copy-start(bf16[512,512]{1,0:T(8,128)(2,1)} %param.12) | copy-start | bytes 1572868
  305.4 209.5 %all-to-all-start.1 = ((bf16[48,8,16384]{2,0,1:T(8,128)(2,1)}), bf16[48,8,16384]{2,0,1:T(8,128)(2,1)}, u32[]{:S(2)}, u32[]{:S(2)}) async-start(bf16[48,8,16384]{2,0,1:T(8,128)(2,1)} %copy.75), calls=%async_computation.1 | async-start | bytes 25165824 | tf_op jit(solution)/shard_map/all_to_all | solution.py:66
  514.9 235.9 %all-to-all-start.3 = ((bf16[48,8,16384]{2,0,1:T(8,128)(2,1)}), bf16[48,8,16384]{2,0,1:T(8,128)(2,1)}, u32[]{:S(2)}, u32[]{:S(2)}) async-start(bf16[48,8,16384]{2,0,1:T(8,128)(2,1)} %copy.80), calls=%async_computation.3 | async-start | bytes 25165824 | tf_op jit(solution)/shard_map/all_to_all | solution.py:69
  520.3 224.3 %all-reduce.3.cloned.1.call-start = ((), (), s32[]{:S(2)}) async-start(), calls=%async_computation.4 | async-start | bytes 5242880 | tf_op jit(solution)/shard_map/psum | solution.py:88
  564.6 106.4 %copy-start.8 = (f32[48,512]{1,0:T(8,128)S(1)}, f32[48,512]{1,0:T(8,128)}, u32[]{:S(2)}) copy-start(f32[48,512]{1,0:T(8,128)} %get-tuple-element.44) | copy-start | bytes 294916
  750.8 12.8 %copy-start.5 = (bf16[512,512]{1,0:T(8,128)(2,1)S(1)}, bf16[512,512]{1,0:T(8,128)(2,1)}, u32[]{:S(2)}) copy-start(bf16[512,512]{1,0:T(8,128)(2,1)} %param.15) | copy-start | bytes 1572868
  862.2 10.5 %copy-start.1 = (f32[384,512]{1,0:T(8,128)S(1)}, f32[384,512]{1,0:T(8,128)}, u32[]{:S(2)}) copy-start(f32[384,512]{1,0:T(8,128)} %param.16) | copy-start | bytes 2359300
Sparse Core Ops, SparseCore 0:
  564.7 179.7 all-reduce.2
where the time goes:
time: 894 us; the launch traced here: 880 us
  local copies, waits for them, and re-layouts  271 us (30%)
  blocking collectives  243 us (27%)
  matrix products  226 us (25%)
  waiting for transfers between devices  77.1 us (9%)
  other arithmetic  31.9 us (4%)
  starting transfers between devices  16.1 us (2%)
  between operations  14.5 us (2%)
    all_to_all x1, blocking collectives, local(): lax.all_to_all(up_gate, 'seq', split_axis=0, concat_axis=1, tiled=True)  144 us
    all_gather x1, blocking collectives, local(): lax.all_gather(rows_part, 'seq', axis=0, tiled=True)  89.7 us
    dot_general x1, matrix products, local(): jnp.einsum('cij,jk->cik', second_rows.reshape(width, rows_local, P2), fac...  65.3 us
    psum x1, waiting for transfers between devices, local(): lax.psum((grad_one, grad_two, grad_three, grad_four), ('seq', 'ch'))  62.6 us
    unnamed x23, local copies, waits for them, and re-layouts  47.1 us
    all_to_all x2, local copies, waits for them, and re-layouts, local(): lax.all_to_all(second.reshape(several, P1 * P2), 'seq', split_axis=1, con...  45.5 us
    all_to_all x2, local copies, waits for them, and re-layouts, local(): lax.all_to_all(local_input.reshape(several, P1 * P2), 'seq', split_axis=1...  34.3 us
    convert_element_type x1, local copies, waits for them, and re-layouts, local(): upstream.reshape(width, rows_local, P2).astype(flt) * final_prod  24.6 us
  transfers between devices with their start and end apart: 4, of which 2 were waited for; matrix products, arithmetic and copies ran while one was open for 40% of the time, Pallas kernels for 0%

commit v1 on v0

--- a/solution.py
+++ b/solution.py
@@ -7,6 +7,24 @@
 P1 = 256
 P2 = 512
 C = 1536
+
+
+def order_vector(u_in, bus_axis, dim_i):
+    windows = [u_in]
+    workers = jax.lax.axis_size(bus_axis)
+    for t in range(1, workers):
+        windows.append(
+            jax.lax.ppermute(
+                windows[t - 1],
+                axis_name=bus_axis,
+                perm=[(kk, (kk - 1) % workers) for kk in range(workers)],
+            )
+        )
+    return jnp.roll(
+        jnp.concatenate(windows, axis=dim_i),
+        shift=jax.lax.axis_index(bus_axis) * u_in.shape[dim_i],
+        axis=dim_i,
+    )
 
 
 def local(
@@ -72,7 +90,7 @@
     )
     cols_sum, rows_sum = (
         lax.all_gather(cols_part, "seq", axis=0, tiled=True),
-        lax.all_gather(rows_part, "seq", axis=0, tiled=True),
+        order_vector(rows_part, "seq", 0),
     )
     final_prod = jnp.einsum(
         "cij,jk->cik",

time: 894 us -> 966 us (1.081)
  waiting for transfers between devices: 77.1 us -> 351 us
  blocking collectives: 243 us -> 26.4 us
  starting transfers between devices: 16.1 us -> 40.4 us
  local copies, waits for them, and re-layouts: 271 us -> 260 us
    all_to_all x1 -> x0, blocking collectives: 144 us -> none  [local(): lax.all_to_all(up_gate, 'seq', split_axis=0, concat_axis=1, tiled=True)]
    all_to_all x1, waiting for transfers between devices: 14.5 us -> 126 us  [local(): lax.all_to_all(inputs, 'seq', split_axis=0, concat_axis=1, tiled=True)]
    ppermute x0 -> x7, waiting for transfers between devices: none -> 105 us  [order_vector(): jax.lax.ppermute(windows[t - 1], axis_name=bus_axis, perm=[(kk, (kk - 1)...]
    all_gather x1 -> x0, blocking collectives: 89.7 us -> none  [local(): lax.all_gather(rows_part, 'seq', axis=0, tiled=True)]
    all_to_all x0 -> x1, waiting for transfers between devices: none -> 61.9 us  [local(): lax.all_to_all(up_gate, 'seq', split_axis=0, concat_axis=1, tiled=True)]
    ppermute x0 -> x7, starting transfers between devices: none -> 18.8 us  [order_vector(): jax.lax.ppermute(windows[t - 1], axis_name=bus_axis, perm=[(kk, (kk - 1)...]
    all_gather x1, blocking collectives: 9.24 us -> 26.4 us  [local(): lax.all_gather(cols_part, 'seq', axis=0, tiled=True)]
    all_to_all x2, local copies, waits for them, and re-layouts: 45.5 us -> 34 us  [local(): lax.all_to_all(second.reshape(several, P1 * P2), 'seq', split_axis=1, con...]
  transfers between devices with their start and end apart: 4 -> 12, of which waited for: 2 -> 9; matrix products, arithmetic and copies ran while one was open for 40% -> 27% of each run, Pallas kernels for 0% -> 0%
where the time goes in v1:
time: 966 us; the launch traced here: 952 us
  waiting for transfers between devices  351 us (36%)
  local copies, waits for them, and re-layouts  260 us (27%)
  matrix products  225 us (23%)
  starting transfers between devices  40.4 us (4%)
  other arithmetic  35.4 us (4%)
  blocking collectives  26.4 us (3%)
  between operations  14.6 us (2%)
    all_to_all x1, waiting for transfers between devices, local(): lax.all_to_all(inputs, 'seq', split_axis=0, concat_axis=1, tiled=True)  126 us
    ppermute x7, waiting for transfers between devices, order_vector(): jax.lax.ppermute(windows[t - 1], axis_name=bus_axis, perm=[(kk, (kk - 1)...  105 us
    dot_general x1, matrix products, local(): jnp.einsum('cij,jk->cik', second_rows.reshape(width, rows_local, P2), fac...  65.3 us
    all_to_all x1, waiting for transfers between devices, local(): lax.all_to_all(up_gate, 'seq', split_axis=0, concat_axis=1, tiled=True)  61.9 us
    psum x1, waiting for transfers between devices, local(): lax.psum((grad_one, grad_two, grad_three, grad_four), ('seq', 'ch'))  58.3 us
    unnamed x36, local copies, waits for them, and re-layouts  47.1 us
    all_to_all x2, local copies, waits for them, and re-layouts, local(): lax.all_to_all(local_input.reshape(several, P1 * P2), 'seq', split_axis=1...  34 us
    all_to_all x2, local copies, waits for them, and re-layouts, local(): lax.all_to_all(second.reshape(several, P1 * P2), 'seq', split_axis=1, con...  34 us
  transfers between devices with their start and end apart: 12, of which 9 were waited for; matrix products, arithmetic and copies ran while one was open for 27% of the time, Pallas kernels for 0%

profile of v1, /device:TPU:0, one launch (start us, length us, event | category | flops | bytes accessed | tf_op | source)
XLA Modules:
  0.0 952.4 jit_solution(13539324114695081341)
XLA Ops:
  7.2 5.5 all-to-all-start.2
  12.7 13.8 %multiply_convert_fusion.4 = bf16[384,16384]{1,0:T(8,128)(2,1)} fusion(bf16[384,16384]{1,0:T(8,128)(2,1)} %param.10, bf16[384,16384]{1,0:T(8,128)(2,1)} %param.11), kind=kLoop, calls=%fused_computation.9 | loop fusion | flops 25165824 | bytes 37748736 | tf_op jit(solution)/shard_map/convert_element_type | solution.py:47
  26.5 125.9 %all-to-all-done.2 = bf16[8,48,16384]{2,1,0:T(8,128)(2,1)} async-done(((bf16[8,48,16384]{2,1,0:T(8,128)(2,1)}), bf16[8,48,16384]{2,1,0:T(8,128)(2,1)}, u32[]{:S(2)}, u32[]{:S(2)}) %all-to-all-start.2) | async-done | bytes 12582944 | tf_op jit(solution)/shard_map/all_to_all | solution.py:49
  152.4 5.3 all-to-all-start
  157.8 17.6 %copy.76 = f32[384,16384]{0,1:T(8,128)} copy(bf16[384,16384]{1,0:T(8,128)(2,1)} %param.11) | data formatting | bytes 37748736 | tf_op jit(solution)/shard_map/convert_element_type | solution.py:47
  175.4 24.7 %copy.82 = f32[384,32,512]{2,0,1:T(8,128)} copy(f32[384,32,512]{0,2,1:T(8,128)} %bitcast.80) | data formatting | bytes 50331648 | tf_op jit(solution)/shard_map/convert_element_type | solution.py:102
  200.9 14.4 %copy.77 = bf16[48,8,16384]{2,1,0:T(8,128)(2,1)} copy(bf16[48,8,16384]{2,0,1:T(8,128)(2,1)} %bitcast.12) | data formatting | bytes 25165824 | tf_op jit(solution)/shard_map/all_to_all | solution.py:49
  215.3 19.5 %reshape.53 = bf16[48,256,512]{2,1,0:T(8,128)(2,1)} reshape(bf16[48,8,16384]{2,1,0:T(8,128)(2,1)} %copy.77) | data formatting | bytes 25165824 | tf_op jit(solution)/shard_map/reshape | solution.py:56
  234.9 61.9 %all-to-all-done = bf16[8,48,16384]{2,1,0:T(8,128)(2,1)} async-done(((bf16[8,48,16384]{2,1,0:T(8,128)(2,1)}), bf16[8,48,16384]{2,1,0:T(8,128)(2,1)}, u32[]{:S(2)}, u32[]{:S(2)}) %all-to-all-start) | async-done | bytes 12582944 | tf_op jit(solution)/shard_map/all_to_all | solution.py:50
  296.7 14.4 %copy.71 = bf16[48,8,16384]{2,1,0:T(8,128)(2,1)} copy(bf16[48,8,16384]{2,0,1:T(8,128)(2,1)} %bitcast.1) | data formatting | bytes 25165824 | tf_op jit(solution)/shard_map/all_to_all | solution.py:50
  311.1 19.5 %reshape.52 = bf16[48,256,512]{2,1,0:T(8,128)(2,1)} reshape(bf16[48,8,16384]{2,1,0:T(8,128)(2,1)} %copy.71) | data formatting | bytes 25165824 | tf_op jit(solution)/shard_map/reshape | solution.py:57
  330.7 11.6 %convolution_convert_fusion.1 = bf16[48,256,512]{2,1,0:T(8,128)(2,1)S(1)} fusion(bf16[48,256,512]{2,1,0:T(8,128)(2,1)} %reshape.52, bf16[512,512]{1,0:T(8,128)(2,1)S(1)} %copy-done.4), kind=kOutput, calls=%fused_computation.19 | convolution fusion | flops 6448742400 | bytes 25690112 | tf_op jit(solution)/shard_map/cik,jk->cij/dot_general | solution.py:66
  342.3 4.5 copy-done.2
  346.7 10.1 %fusion.39 = f32[48,512,256]{2,1,0:T(8,128)} fusion(bf16[48,256,512]{2,1,0:T(8,128)(2,1)S(1)} %convolution_convert_fusion.1, bf16[256,256]{1,0:T(8,128)(2,1)S(1)} %copy-done.7), kind=kOutput, calls=%fused_computation.39 | convolution fusion | flops 3221225472 | bytes 37879808 | tf_op jit(solution)/shard_map/ki,ckj->cij/dot_general | solution.py:70
  356.8 14.8 %convolution_convert_fusion = bf16[48,512,256]{1,2,0:T(8,128)(2,1)} fusion(f32[48,512,256]{2,1,0:T(8,128)} %fusion.39, f32[48,256]{1,0:T(8,128)S(1)} %constant_dynamic-slice_fusion.1, bf16[256,256]{1,0:T(8,128)(2,1)S(1)} %copy-done.6), kind=kOutput, calls=%fused_computation.17 | convolution fusion | flops 3240099840 | bytes 37928960 | tf_op jit(solution)/shard_map/ki,ckj->cij/dot_general | solution.py:74
  371.6 14.6 %fusion.10 = bf16[48,256,512]{2,1,0:T(8,128)(2,1)} fusion(bf16[48,512,256]{1,2,0:T(8,128)(2,1)} %convolution_convert_fusion, f32[48,512]{1,0:T(8,128)S(1)} %constant_dynamic-slice_fusion, bf16[512,512]{1,0:T(8,128)(2,1)S(1)} %copy-done.3), kind=kOutput, calls=%fused_computation.18 | convolution fusion | flops 6467616768 | bytes 25788416 | tf_op jit(solution)/shard_map/cik,jk->cij/dot_general | solution.py:80
  386.2 19.5 %all_to_all.53 = bf16[48,8,16384]{2,1,0:T(8,128)(2,1)} reshape(bf16[48,256,512]{2,1,0:T(8,128)(2,1)} %fusion.10) | data formatting | bytes 25165824 | tf_op jit(solution)/shard_map/all_to_all | solution.py:84
  405.7 14.5 %copy.75 = bf16[48,8,16384]{2,0,1:T(8,128)(2,1)} copy(bf16[48,8,16384]{2,1,0:T(8,128)(2,1)} %all_to_all.53) | data formatting | bytes 25165824 | tf_op jit(solution)/shard_map/all_to_all | solution.py:84
  420.2 5.3 all-to-all-start.1
  425.6 18.4 %fusion.1 = (f32[48,512]{1,0:T(8,128)S(1)}, f32[48,256,512]{2,1,0:T(8,128)}) fusion(bf16[48,512,256]{1,2,0:T(8,128)(2,1)} %convolution_convert_fusion, bf16[48,256,512]{2,1,0:T(8,128)(2,1)} %reshape.53, bf16[512,512]{1,0:T(8,128)(2,1)S(1)} %copy-done.3), kind=kOutput, calls=%fused_computation.3 | convolution fusion | flops 6461300736 | bytes 50954240 | tf_op jit(solution)/shard_map/cij,jk->cik/dot_general | solution.py:58
  443.9 16.2 %fusion.21 = f32[48,512,256]{2,1,0:T(8,128)} fusion(f32[48,256,512]{2,1,0:T(8,128)} %get-tuple-element.45, f32[48,512]{1,0:T(8,128)S(1)} %constant_dynamic-slice_fusion, bf16[256,256]{1,0:T(8,128)(2,1)S(1)} %copy-done.6), kind=kOutput, calls=%fused_computation.22 | convolution fusion | flops 3233808384 | bytes 50561024 | tf_op jit(solution)/shard_map/ki,cij->ckj/dot_general | solution.py:60
  460.1 14.5 %convert_bitcast_fusion = bf16[48,256,512]{1,2,0:T(8,128)(2,1)} fusion(f32[48,512,256]{2,1,0:T(8,128)} %fusion.21, f32[48,256]{1,0:T(8,128)S(1)} %constant_dynamic-slice_fusion.1, bf16[256,256]{1,0:T(8,128)(2,1)S(1)} %copy-done.7), kind=kOutput, calls=%fused_computation.14 | convolution fusion | flops 3240099840 | bytes 37928960 | tf_op jit(solution)/shard_map/ki,cij->ckj/dot_general | solution.py:62
  474.6 16.7 %copy.79 = bf16[48,256,512]{2,1,0:T(8,128)(2,1)} copy(bf16[48,256,512]{1,2,0:T(8,128)(2,1)} %convert_bitcast_fusion) | data formatting | bytes 25165824 | tf_op jit(solution)/shard_map/convert_element_type | solution.py:62
  491.3 19.6 %all_to_all.60 = bf16[48,8,16384]{2,1,0:T(8,128)(2,1)} reshape(bf16[48,256,512]{2,1,0:T(8,128)(2,1)} %copy.79) | data formatting | bytes 25165824 | tf_op jit(solution)/shard_map/all_to_all | solution.py:87
  510.8 14.5 %copy.80 = bf16[48,8,16384]{2,0,1:T(8,128)(2,1)} copy(bf16[48,8,16384]{2,1,0:T(8,128)(2,1)} %all_to_all.60) | data formatting | bytes 25165824 | tf_op jit(solution)/shard_map/all_to_all | solution.py:87
  525.3 16.2 %multiply_reduce_fusion = f32[48,256]{1,0:T(8,128)S(1)} fusion(f32[48,512,256]{2,1,0:T(8,128)} %fusion.39, f32[48,512,256]{2,1,0:T(8,128)} %fusion.21), kind=kLoop, calls=%fused_computation.4 | loop fusion | flops 12570624 | bytes 50380800 | tf_op jit(solution)/shard_map/reduce_sum | solution.py:71
  541.5 2.6 collective-permute-start
  544.1 26.4 %all_gather.3 = f32[384,512]{1,0:T(8,128)S(1)} all-gather(f32[48,512]{1,0:T(8,128)S(1)} %get-tuple-element.44), channel_id=1, replica_groups=mesh['seq'=8,'ch'=4] {'seq'}, dimensions={0}, use_global_device_ids=true | all-gather | bytes 884736 | tf_op jit(solution)/shard_map/all_gather | solution.py:92
  570.4 15.9 %fusion.28 = f32[256,256]{1,0:T(8,128)} fusion(bf16[48,256,512]{2,1,0:T(8,128)(2,1)} %copy-done.2, f32[48,512,256]{2,1,0:T(8,128)} %fusion.21, f32[48,256]{1,0:T(8,128)S(1)} %constant_dynamic-slice_fusion.1), kind=kOutput, calls=%fused_computation.26 | convolution fusion | flops 3233808384 | bytes 38060032 | tf_op jit(solution)/shard_map/ckj,cij->ki/dot_general | solution.py:69
  586.3 5.4 all-to-all-start.3
  592.7 14.1 %fusion.22 = f32[512,512]{0,1:T(8,128)} fusion(bf16[48,256,512]{2,1,0:T(8,128)(2,1)} %reshape.53, bf16[48,512,256]{1,2,0:T(8,128)(2,1)} %convolution_convert_fusion, f32[48,512]{1,0:T(8,128)S(1)} %constant_dynamic-slice_fusion), kind=kOutput, calls=%fused_computation.23 | convolution fusion | flops 6461325312 | bytes 26312704 | tf_op jit(solution)/shard_map/cij,cik->jk/dot_general | solution.py:79
  606.7 12.6 %convolution_bitcast_fusion = f32[512,512]{0,1:T(8,128)} fusion(bf16[48,256,512]{1,2,0:T(8,128)(2,1)} %convert_bitcast_fusion, bf16[48,256,512]{2,1,0:T(8,128)(2,1)} %reshape.52), kind=kOutput, calls=%fused_computation.24 | convolution fusion | flops 6442450944 | bytes 26214400 | tf_op jit(solution)/shard_map/cij,cik->jk/dot_general | solution.py:65
  619.4 17.6 %fusion.25 = f32[256,256]{1,0:T(8,128)} fusion(f32[48,256,512]{2,1,0:T(8,128)} %get-tuple-element.45, f32[48,512]{1,0:T(8,128)S(1)} %constant_dynamic-slice_fusion, f32[48,512,256]{2,1,0:T(8,128)} %fusion.39, f32[48,256]{1,0:T(8,128)S(1)} %constant_dynamic-slice_fusion.1), kind=kOutput, calls=%fused_computation.25 | convolution fusion | flops 3246391296 | bytes 50741248 | tf_op jit(solution)/shard_map/ckj,cij->ki/dot_general | solution.py:73
  637.0 2.6 collective-permute-start.1
  639.5 95.9 %collective-permute-done.1 = f32[48,256]{1,0:T(8,128)S(1)} collective-permute-done((f32[48,256]{1,0:T(8,128)S(1)}, f32[48,256]{1,0:T(8,128)S(1)}, u32[]{:S(2)}, u32[]{:S(2)}) %collective-permute-start.1) | collective-permute-done | bytes 49184 | tf_op jit(solution)/shard_map/ppermute | solution.py:17
  735.4 2.9 collective-permute-start.2
  740.1 2.7 collective-permute-start.3
  744.5 2.7 collective-permute-start.4
  748.9 2.7 collective-permute-start.5
  753.3 2.7 collective-permute-start.6
  758.7 58.3 %all-reduce.3.cloned.1.call-done = (f32[512,512]{0,1:T(8,128)}, f32[256,256]{1,0:T(8,128)}, f32[256,256]{1,0:T(8,128)}, f32[512,512]{0,1:T(8,128)}) async-done(((f32[512,512]{0,1:T(8,128)}, f32[256,256]{1,0:T(8,128)}, f32[256,256]{1,0:T(8,128)}, f32[512,512]{0,1:T(8,128)}), (f32[512,512]{0,1:T(8,128)}, f32[256,256]{1,0:T(8,128)}, f32[256,256]{1,0:T(8,128)}, ...) | async-done | bytes 2621456 | tf_op jit(solution)/shard_map/psum | solution.py:106
  817.0 1.8 broadcast_multiply_fusion
  821.4 1.9 broadcast_multiply_fusion.3
  823.3 12.8 %copy.101 = bf16[48,8,32,512]{3,2,1,0:T(8,128)(2,1)} copy(bf16[48,8,32,512]{3,1,2,0:T(8,128)(2,1)} %bitcast.26) | data formatting | bytes 25165824
  836.1 65.3 %multiply_convert_fusion = bf16[384,32,512]{2,0,1:T(8,128)(2,1)} fusion(f32[384,32,512]{2,0,1:T(8,128)} %copy.82, bf16[384,32,512]{2,1,0:T(8,128)(2,1)} %bitcast.81, bf16[512,512]{1,0:T(8,128)(2,1)S(1)} %copy-done.5), kind=kOutput, calls=%fused_computation.5 | convolution fusion | flops 6455033856 | bytes 50855936 | tf_op jit(solution)/shard_map/cij,jk->cik/dot_general | solution.py:95
  901.4 16.6 %copy.83 = bf16[384,32,512]{0,2,1:T(8,128)(2,1)} copy(bf16[384,32,512]{2,0,1:T(8,128)(2,1)} %multiply_convert_fusion) | data formatting | bytes 25165824 | tf_op jit(solution)/shard_map/convert_element_type | solution.py:103
  918.0 16.6 %copy.88 = bf16[384,16384]{1,0:T(8,128)(2,1)} copy(bf16[384,16384]{0,1:T(8,128)(2,1)} %bitcast.82) | data formatting | bytes 25165824
  934.6 10.5 %copy.126 = bf16[384,16384]{1,0:T(8,128)(2,1)} copy(bf16[384,16384]{1,0:T(8,128)(2,1)} %bitcast.9) | data formatting | bytes 25165824
  (47 shorter events, 14.1 us)
Async XLA Ops:
  7.2 193.7 %copy-start = (f32[384,512]{1,0:T(8,128)S(1)}, f32[384,512]{1,0:T(8,128)}, u32[]{:S(2)}) copy-start(f32[384,512]{1,0:T(8,128)} %param.16) | copy-start | bytes 2359300
  7.2 145.2 %all-to-all-start.2 = ((bf16[8,48,16384]{2,1,0:T(8,128)(2,1)}), bf16[8,48,16384]{2,1,0:T(8,128)(2,1)}, u32[]{:S(2)}, u32[]{:S(2)}) async-start(bf16[8,48,16384]{2,1,0:T(8,128)(2,1)} %bitcast.84), calls=%async_computation.2 | async-start | bytes 25165824 | tf_op jit(solution)/shard_map/all_to_all | solution.py:49
  152.4 144.3 %all-to-all-start = ((bf16[8,48,16384]{2,1,0:T(8,128)(2,1)}), bf16[8,48,16384]{2,1,0:T(8,128)(2,1)}, u32[]{:S(2)}, u32[]{:S(2)}) async-start(bf16[8,48,16384]{2,1,0:T(8,128)(2,1)} %bitcast.83), calls=%async_computation | async-start | bytes 25165824 | tf_op jit(solution)/shard_map/all_to_all | solution.py:50
  311.1 19.5 %copy-start.4 = (bf16[512,512]{1,0:T(8,128)(2,1)S(1)}, bf16[512,512]{1,0:T(8,128)(2,1)}, u32[]{:S(2)}) copy-start(bf16[512,512]{1,0:T(8,128)(2,1)} %param.15) | copy-start | bytes 1572868
  330.7 16.1 %copy-start.7 = (bf16[256,256]{1,0:T(8,128)(2,1)S(1)}, bf16[256,256]{1,0:T(8,128)(2,1)}, u32[]{:S(2)}) copy-start(bf16[256,256]{1,0:T(8,128)(2,1)} %param.14) | copy-start | bytes 393220
  342.3 4.5 copy-start.2
  346.7 10.1 %copy-start.6 = (bf16[256,256]{1,0:T(8,128)(2,1)S(1)}, bf16[256,256]{1,0:T(8,128)(2,1)}, u32[]{:S(2)}) copy-start(bf16[256,256]{1,0:T(8,128)(2,1)} %param.13) | copy-start | bytes 393220
  356.8 14.8 %copy-start.3 = (bf16[512,512]{1,0:T(8,128)(2,1)S(1)}, bf16[512,512]{1,0:T(8,128)(2,1)}, u32[]{:S(2)}) copy-start(bf16[512,512]{1,0:T(8,128)(2,1)} %param.12) | copy-start | bytes 1572868
  420.2 166.1 %all-to-all-start.1 = ((bf16[48,8,16384]{2,0,1:T(8,128)(2,1)}), bf16[48,8,16384]{2,0,1:T(8,128)(2,1)}, u32[]{:S(2)}, u32[]{:S(2)}) async-start(bf16[48,8,16384]{2,0,1:T(8,128)(2,1)} %copy.75), calls=%async_computation.1 | async-start | bytes 25165824 | tf_op jit(solution)/shard_map/all_to_all | solution.py:84
  541.5 95.5 %collective-permute-start = (f32[48,256]{1,0:T(8,128)S(1)}, f32[48,256]{1,0:T(8,128)S(1)}, u32[]{:S(2)}, u32[]{:S(2)}) collective-permute-start(f32[48,256]{1,0:T(8,128)S(1)} %multiply_reduce_fusion), channel_id=1, source_target_pairs={{0,28},{4,0},{8,4},{12,8},{16,12},{20,16},{24,20},{28,24},{1,29},{... | collective-permute-start | bytes 147464 | tf_op jit(solution)/shard_map/ppermute | solution.py:17
  586.3 237.0 %all-to-all-start.3 = ((bf16[48,8,16384]{2,0,1:T(8,128)(2,1)}), bf16[48,8,16384]{2,0,1:T(8,128)(2,1)}, u32[]{:S(2)}, u32[]{:S(2)}) async-start(bf16[48,8,16384]{2,0,1:T(8,128)(2,1)} %copy.80), calls=%async_computation.3 | async-start | bytes 25165824 | tf_op jit(solution)/shard_map/all_to_all | solution.py:87
  591.7 225.4 %all-reduce.3.cloned.1.call-start = ((), (), s32[]{:S(2)}) async-start(), calls=%async_computation.4 | async-start | bytes 5242880 | tf_op jit(solution)/shard_map/psum | solution.py:106
  637.0 98.5 %collective-permute-start.1 = (f32[48,256]{1,0:T(8,128)S(1)}, f32[48,256]{1,0:T(8,128)S(1)}, u32[]{:S(2)}, u32[]{:S(2)}) collective-permute-start(f32[48,256]{1,0:T(8,128)S(1)} %collective-permute-done), channel_id=1, source_target_pairs={{0,28},{4,0},{8,4},{12,8},{16,12},{20,16},{24,20},{28,24},{1,29},{... | collective-permute-start | bytes 147464 | tf_op jit(solution)/shard_map/ppermute | solution.py:17
  735.4 4.7 collective-permute-start.2
  740.1 4.4 collective-permute-start.3
  744.5 4.4 collective-permute-start.4
  748.9 4.4 collective-permute-start.5
  753.3 4.5 collective-permute-start.6
  823.3 12.8 %copy-start.5 = (bf16[512,512]{1,0:T(8,128)(2,1)S(1)}, bf16[512,512]{1,0:T(8,128)(2,1)}, u32[]{:S(2)}) copy-start(bf16[512,512]{1,0:T(8,128)(2,1)} %param.15) | copy-start | bytes 1572868
  934.6 10.5 %copy-start.1 = (f32[384,512]{1,0:T(8,128)S(1)}, f32[384,512]{1,0:T(8,128)}, u32[]{:S(2)}) copy-start(f32[384,512]{1,0:T(8,128)} %param.16) | copy-start | bytes 2359300
Sparse Core Ops, SparseCore 0:
  637.1 179.8 all-reduce.2
